TPU v7x, 256 devices: a whole 4x4x8 slice. The times are simulated.
256 devices in a mesh: sub: 2 (over x_lo), row: 8 (over y, x_hi), col: 16 (over z, core).
Axes of the slice: x: 4 (x_hi: 2, x_lo: 2; x = x_hi * 2 + x_lo), y: 4, z: 8, core: 2. Of those that a mesh axis runs over, the one named last changes fastest.
Arguments:
- front: float32 [10240, 10240], P(('sub', 'row'), 'col')
- children: float32 [4, 6144, 6144], P('sub', 'row', 'col')
- child_maps: int32 [4, 48], replicated, may hold values from 0 to 79, as said below
Outputs:
- factored: float32 [10240, 10240], P(('sub', 'row'), 'col')
Inputs may be any that keep to these rules, and one draw needn't show every extreme that they name: `child_maps`: each row holds 48 different parent block numbers, and entry i leaves the same remainder as i on division by 16. Child 0 sends its block 0 to parent block 0, child 1 its last block to parent block 79.
All inputs are finite; a program needn't handle non-finite values.
Results may differ from a plain program's by a relative error of at most 0.0001.
Values sent between devices are 32-bit elements; how exact they have to be, the bound alone decides.
A program may use at most 64 MiB of HBM per device.

v0:
```python
import jax
import jax.numpy as jnp
from jax import lax
from jax.sharding import PartitionSpec as P

BS = 128
NPB = 3


def from_root(value, axis, source):
    kept = jnp.where(lax.axis_index(axis) == source, value, 0).astype(value.dtype)
    return lax.psum(kept, axis)


def body(front, children, child_maps):
    n_sub = lax.axis_size("sub")
    n_row = lax.axis_size("row")
    n_col = lax.axis_size("col")
    rowdev = n_sub * n_row
    sub_idx = lax.axis_index("sub")
    row_idx = lax.axis_index("row")
    col_idx = lax.axis_index("col")
    dev_row = sub_idx * n_row + row_idx
    local_rows, local_cols = front.shape
    row_blocks = local_rows // BS
    col_blocks = local_cols // BS
    per_group, child_rows, child_cols = children.shape
    half_rows = child_rows // BS // n_sub
    child_cblocks = child_cols // BS
    highest = lax.Precision.HIGHEST
    col_pick = jnp.arange(child_cblocks, dtype=jnp.int32) * n_col + col_idx
    pieces = children.reshape(per_group, half_rows, n_sub, BS, child_cols)
    arrived = lax.all_to_all(pieces, "sub", split_axis=2, concat_axis=0, tiled=True)
    arrived = arrived.reshape(per_group * n_sub, half_rows, BS, child_cblocks, BS)
    row_pick = (jnp.arange(half_rows, dtype=jnp.int32) * n_sub + sub_idx) * n_row + row_idx
    row_dest = child_maps[:, row_pick] // rowdev
    col_dest = child_maps[:, col_pick] // n_col
    row_hot = (row_dest[..., None] == jnp.arange(row_blocks, dtype=jnp.int32)).astype(jnp.float32)
    col_hot = (col_dest[..., None] == jnp.arange(col_blocks, dtype=jnp.int32)).astype(jnp.float32)
    placed = jnp.einsum("cua,cuxmy->caxmy", row_hot, arrived, precision=highest)
    extended = jnp.einsum("caxmy,cmb->axby", placed, col_hot, precision=highest)
    assembled = front + extended.reshape(local_rows, local_cols)
    row_block = jnp.arange(local_rows, dtype=jnp.int32) // BS * rowdev + dev_row
    col_block = jnp.arange(local_cols, dtype=jnp.int32) // BS * n_col + col_idx
    col_ratio = n_col // rowdev
    identity = jnp.eye(BS, dtype=jnp.float32)

    def eliminate(section, matrix):
        section = section.astype(jnp.int32)
        owner_row = section % rowdev
        local_row = section // rowdev
        owner_col = section % n_col
        local_col = section // n_col
        corner = lax.dynamic_slice(matrix, (local_row * BS, local_col * BS), (BS, BS))
        diag_block = from_root(corner, ("sub", "row", "col"), owner_row * n_col + owner_col)
        factor = jnp.linalg.cholesky(diag_block)
        inverse = jax.scipy.linalg.solve_triangular(factor, identity, lower=True)
        column = lax.dynamic_slice_in_dim(matrix, local_col * BS, BS, 1)
        column_in = from_root(column, "col", owner_col)
        panel_rows = jnp.dot(column_in, inverse.T, precision=highest)
        below_mask = (row_block > section)[:, None]
        left_factor = jnp.where(below_mask, panel_rows, 0.0)
        right_mask = col_block > section
        grouped = panel_rows.reshape(col_blocks, col_ratio, BS, BS)
        chosen = lax.dynamic_index_in_dim(grouped, col_idx // rowdev, 1, keepdims=False)
        partner = from_root(chosen, ("sub", "row"), col_idx % rowdev)
        partner = jnp.where(right_mask.reshape(col_blocks, BS)[:, :, None], partner, 0.0)
        update = lax.dot_general(
            left_factor,
            partner.reshape(local_cols, BS),
            (((1,), (1,)), ((), ())),
            precision=highest,
        )
        matrix = matrix - update
        lower_tile = jnp.tile(jnp.tril(factor), (row_blocks, 1))
        written = jnp.where(
            below_mask, panel_rows, jnp.where((row_block == section)[:, None], lower_tile, 0.0)
        )
        current = lax.dynamic_slice_in_dim(matrix, local_col * BS, BS, 1)
        matrix = lax.dynamic_update_slice_in_dim(
            matrix, jnp.where(col_idx == owner_col, written, current), local_col * BS, 1
        )
        strip_now = lax.dynamic_slice_in_dim(matrix, local_row * BS, BS, 0)
        cleared = jnp.where((dev_row == owner_row) & right_mask[None, :], 0.0, strip_now)
        return lax.dynamic_update_slice_in_dim(matrix, cleared, local_row * BS, 0)

    return lax.fori_loop(0, NPB, eliminate, assembled)


def solution(mesh):
    return jax.shard_map(
        body,
        mesh=mesh,
        in_specs=(P(("sub", "row"), "col"), P("sub", "row", "col"), P()),
        out_specs=P(("sub", "row"), "col"),
        check_vma=False,
    )
```

profile of v0, /device:TPU:2, one launch (start us, length us, event | category | flops | bytes accessed | tf_op | source)
XLA Modules:
  0.0 1432.7 jit_solution(5333584483358286880)
XLA Ops:
  6.5 3.2 copy.23
  9.8 6.2 all-to-all-start
  17.3 22.3 %all-to-all-done = f32[2,3,2,128,384]{4,3,1,0,2:T(8,128)S(1)} async-done(((f32[2,3,2,128,384]{4,3,1,0,2:T(8,128)}), f32[2,3,2,128,384]{4,3,1,0,2:T(8,128)S(1)}, u32[]{:S(2)}, u32[]{:S(2)}) %all-to-all-start) | async-done | bytes 2359328 | tf_op jit(solution)/shard_map/all_to_all | solution.py:33
  39.6 2.0 copy.24
  41.6 3.2 copy.25
  44.7 4.0 fusion.30
  48.8 6.3 fusion.27
  55.6 1369.4 %while.17 = (s32[]{:T(128)}, f32[640,640]{1,0:T(8,128)S(1)}, s32[]{:T(128)}, s32[]{:T(128)}, s32[]{:T(128)}, /*index=5*/s32[]{:T(128)}, u32[]{:T(128)}, u32[]{:T...) while((s32[]{:T(128)}, f32[640,640]{1,0:T(8,128)S(1)}, ...), condition=%wide.region_6.7_spmd.clone.clone, body=%wide.region_0.6_spmd.clone.clone.sunk | while | flops 781671040 | bytes 13246939 | solution.py:87
  57.4 250.0 %all-reduce.6.cloned.1.call-done = f32[128,128]{1,0:T(8,128)} async-done(((f32[128,128]{1,0:T(8,128)}), f32[128,128]{1,0:T(8,128)}) %all-reduce.6.cloned.1.call-update) | async-done | bytes 65552 | tf_op jit(solution)/shard_map/while/body/eval_jaxpr/psum | solution.py:12
  309.3 11.7 cholesky.85
  322.4 9.8 custom-call.28
  332.5 82.9 %all-reduce.4.cloned.1.call-done = f32[640,128]{1,0:T(8,128)} async-done(((f32[640,128]{1,0:T(8,128)}), f32[640,128]{1,0:T(8,128)}) %all-reduce.4.cloned.1.call-update) | async-done | bytes 327696 | tf_op jit(solution)/shard_map/while/body/eval_jaxpr/psum | solution.py:12
  415.4 2.1 broadcast_select_fusion.4
  418.2 94.0 %all-reduce.8.cloned.1.call-done = f32[5,128,128]{2,1,0:T(8,128)} async-done(((f32[5,128,128]{2,1,0:T(8,128)}), f32[5,128,128]{2,1,0:T(8,128)}) %all-reduce.8.cloned.1.call-update) | async-done | bytes 327696 | tf_op jit(solution)/shard_map/while/body/eval_jaxpr/psum | solution.py:12
  512.2 1.1 broadcast_select_fusion.5
  513.3 2.1 convolution_subtract_fusion.2
  517.4 244.7 %all-reduce.6.cloned.1.call-done = f32[128,128]{1,0:T(8,128)} async-done(((f32[128,128]{1,0:T(8,128)}), f32[128,128]{1,0:T(8,128)}) %all-reduce.6.cloned.1.call-update) | async-done | bytes 65552 | tf_op jit(solution)/shard_map/while/body/eval_jaxpr/psum | solution.py:12
  763.9 11.7 cholesky.85
  777.0 9.8 custom-call.28
  787.1 82.7 %all-reduce.4.cloned.1.call-done = f32[640,128]{1,0:T(8,128)} async-done(((f32[640,128]{1,0:T(8,128)}), f32[640,128]{1,0:T(8,128)}) %all-reduce.4.cloned.1.call-update) | async-done | bytes 327696 | tf_op jit(solution)/shard_map/while/body/eval_jaxpr/psum | solution.py:12
  869.8 2.1 broadcast_select_fusion.4
  872.6 93.9 %all-reduce.8.cloned.1.call-done = f32[5,128,128]{2,1,0:T(8,128)} async-done(((f32[5,128,128]{2,1,0:T(8,128)}), f32[5,128,128]{2,1,0:T(8,128)}) %all-reduce.8.cloned.1.call-update) | async-done | bytes 327696 | tf_op jit(solution)/shard_map/while/body/eval_jaxpr/psum | solution.py:12
  966.5 1.1 broadcast_select_fusion.5
  967.7 2.1 convolution_subtract_fusion.2
  971.7 245.0 %all-reduce.6.cloned.1.call-done = f32[128,128]{1,0:T(8,128)} async-done(((f32[128,128]{1,0:T(8,128)}), f32[128,128]{1,0:T(8,128)}) %all-reduce.6.cloned.1.call-update) | async-done | bytes 65552 | tf_op jit(solution)/shard_map/while/body/eval_jaxpr/psum | solution.py:12
  1218.6 11.7 cholesky.85
  1231.6 9.8 custom-call.28
  1241.7 82.9 %all-reduce.4.cloned.1.call-done = f32[640,128]{1,0:T(8,128)} async-done(((f32[640,128]{1,0:T(8,128)}), f32[640,128]{1,0:T(8,128)}) %all-reduce.4.cloned.1.call-update) | async-done | bytes 327696 | tf_op jit(solution)/shard_map/while/body/eval_jaxpr/psum | solution.py:12
  1324.7 2.1 broadcast_select_fusion.4
  1327.5 94.0 %all-reduce.8.cloned.1.call-done = f32[5,128,128]{2,1,0:T(8,128)} async-done(((f32[5,128,128]{2,1,0:T(8,128)}), f32[5,128,128]{2,1,0:T(8,128)}) %all-reduce.8.cloned.1.call-update) | async-done | bytes 327696 | tf_op jit(solution)/shard_map/while/body/eval_jaxpr/psum | solution.py:12
  1422.6 2.1 convolution_subtract_fusion.2
  1425.0 1.2 copy-done
  (77 shorter events, 20.8 us)
Async XLA Ops:
  9.8 6.2 copy-start.2
  9.8 29.8 %all-to-all-start = ((f32[2,3,2,128,384]{4,3,1,0,2:T(8,128)}), f32[2,3,2,128,384]{4,3,1,0,2:T(8,128)S(1)}, u32[]{:S(2)}, u32[]{:S(2)}) async-start(f32[2,3,2,128,384]{4,3,1,0,2:T(8,128)} %copy.23), calls=%async_computation | async-start | bytes 4718592 | tf_op jit(solution)/shard_map/all_to_all | solution.py:33
  48.7 6.3 copy-start.1
  55.8 251.7 %all-reduce.6.cloned.1.call-start = ((), (), s32[]{:S(2)}) async-start(), calls=%async_computation.2 | async-start | bytes 131072 | tf_op jit(solution)/shard_map/while/body/eval_jaxpr/psum | solution.py:12
  56.5 358.9 %all-reduce.4.cloned.1.call-start = ((), (), s32[]{:S(2)}) async-start(), calls=%async_computation.1 | async-start | bytes 655360 | tf_op jit(solution)/shard_map/while/body/eval_jaxpr/psum | solution.py:12
  57.3 454.9 %all-reduce.8.cloned.1.call-start = ((), (), s32[]{:S(2)}) async-start(), calls=%async_computation.3 | async-start | bytes 655360 | tf_op jit(solution)/shard_map/while/body/eval_jaxpr/psum | solution.py:12
  515.7 246.4 %all-reduce.6.cloned.1.call-start = ((), (), s32[]{:S(2)}) async-start(), calls=%async_computation.2 | async-start | bytes 131072 | tf_op jit(solution)/shard_map/while/body/eval_jaxpr/psum | solution.py:12
  516.5 353.3 %all-reduce.4.cloned.1.call-start = ((), (), s32[]{:S(2)}) async-start(), calls=%async_computation.1 | async-start | bytes 655360 | tf_op jit(solution)/shard_map/while/body/eval_jaxpr/psum | solution.py:12
  517.3 449.2 %all-reduce.8.cloned.1.call-start = ((), (), s32[]{:S(2)}) async-start(), calls=%async_computation.3 | async-start | bytes 655360 | tf_op jit(solution)/shard_map/while/body/eval_jaxpr/psum | solution.py:12
  970.0 246.7 %all-reduce.6.cloned.1.call-start = ((), (), s32[]{:S(2)}) async-start(), calls=%async_computation.2 | async-start | bytes 131072 | tf_op jit(solution)/shard_map/while/body/eval_jaxpr/psum | solution.py:12
  970.8 353.9 %all-reduce.4.cloned.1.call-start = ((), (), s32[]{:S(2)}) async-start(), calls=%async_computation.1 | async-start | bytes 655360 | tf_op jit(solution)/shard_map/while/body/eval_jaxpr/psum | solution.py:12
  971.6 449.9 %all-reduce.8.cloned.1.call-start = ((), (), s32[]{:S(2)}) async-start(), calls=%async_computation.3 | async-start | bytes 655360 | tf_op jit(solution)/shard_map/while/body/eval_jaxpr/psum | solution.py:12
  1425.0 1.2 copy-start
Sparse Core Ops, SparseCore 0:
  62.1 245.3 all-reduce.5
  309.8 105.4 all-reduce.3
  418.6 93.5 all-reduce.7
  521.7 240.3 all-reduce.5
  764.3 105.4 all-reduce.3
  872.9 93.6 all-reduce.7
  976.4 240.3 all-reduce.5
  1219.1 105.4 all-reduce.3
  1327.9 93.5 all-reduce.7
where the time goes:
time: 1430 us
  waiting for transfers between devices  1290 us (90%)
  other arithmetic  82.1 us (6%)
  matrix products  23.7 us (2%)
    psum x9, waiting for transfers between devices, from_root(): return lax.psum(kept, axis)  1270 us
    another operation x9, other arithmetic, eliminate(): factor = jnp.linalg.cholesky(diag_block)  37.3 us
    another operation x9, other arithmetic, eliminate(): inverse = jax.scipy.linalg.solve_triangular(factor, identity, lower=True)  33.3 us
  transfers between devices with their start and end apart: 10, of which 10 were waited for; matrix products, arithmetic and copies ran while one was open for 6% of the time, Pallas kernels for 0%

commit v1 on v0

--- a/solution.py
+++ b/solution.py
@@ -9,7 +9,7 @@
 
 def from_root(value, axis, source):
     kept = jnp.where(lax.axis_index(axis) == source, value, 0).astype(value.dtype)
-    return lax.psum(kept, axis)
+    return jnp.sum(lax.all_gather(kept, axis), axis=0)
 
 
 def body(front, children, child_maps):

time: 1430 us -> 2020 us (1.41)
  waiting for transfers between devices: 1290 us -> 1840 us
  other arithmetic: 82.1 us -> 113 us
    all_gather x0 -> x9, waiting for transfers between devices: none -> 1820 us  [from_root(): return jnp.sum(lax.all_gather(kept, axis), axis=0)]
    psum x9 -> x0, waiting for transfers between devices: 1270 us -> none  [from_root(): return lax.psum(kept, axis)]
    reduce_sum x0 -> x9, other arithmetic: none -> 36.4 us  [from_root(): return jnp.sum(lax.all_gather(kept, axis), axis=0)]
  transfers between devices with their start and end apart: 10 -> 10, of which waited for: 10 -> 10; matrix products, arithmetic and copies ran while one was open for 6% -> 1% of each run, Pallas kernels for 0% -> 0%
where the time goes in v1:
time: 2020 us; the launch traced here: 2010 us
  waiting for transfers between devices  1840 us (91%)
  other arithmetic  113 us (6%)
  matrix products  22.7 us (1%)
    all_gather x9, waiting for transfers between devices, from_root(): return jnp.sum(lax.all_gather(kept, axis), axis=0)  1820 us
  transfers between devices with their start and end apart: 10, of which 10 were waited for; matrix products, arithmetic and copies ran while one was open for 1% of the time, Pallas kernels for 0%

profile of v1, /device:TPU:2, one launch (start us, length us, event | category | flops | bytes accessed | tf_op | source)
XLA Modules:
  0.0 2011.6 jit_solution(423714571600980760)
XLA Ops:
  6.5 3.2 copy.23
  9.8 7.3 all-to-all-start
  18.4 22.4 %all-to-all-done = f32[2,3,2,128,384]{4,3,1,0,2:T(8,128)} async-done(((f32[2,3,2,128,384]{4,3,1,0,2:T(8,128)}), f32[2,3,2,128,384]{4,3,1,0,2:T(8,128)}, u32[]{:S(2)}, u32[]{:S(2)}) %all-to-all-start) | async-done | bytes 2359328 | tf_op jit(solution)/shard_map/all_to_all | solution.py:33
  40.8 3.1 copy.24
  43.9 4.5 copy.25
  48.4 5.9 fusion.28
  54.3 6.3 fusion.25
  61.1 1942.7 %while.17 = (s32[]{:T(128)}, f32[640,640]{1,0:T(8,128)S(1)}, s32[]{:T(128)}, s32[]{:T(128)}, s32[]{:T(128)}, /*index=5*/s32[]{:T(128)}, u32[]{:T(128)}, u32[]{:T...) while((s32[]{:T(128)}, f32[640,640]{1,0:T(8,128)S(1)}, ...), condition=%wide.region_6.7_spmd.clone.clone, body=%wide.region_0.6_spmd.clone.clone.sunk | while | flops 788120576 | bytes 120857072 | solution.py:87
  63.0 49.1 %all-gather.14.cloned.1.call-done = f32[10240,128]{1,0:T(8,128)} async-done(((f32[640,128]{1,0:T(8,128)}), f32[10240,128]{1,0:T(8,128)}) %all-gather.14.cloned.1.call-update) | async-done | bytes 5242896 | tf_op jit(solution)/shard_map/while/body/eval_jaxpr/all_gather | solution.py:12
  112.1 2.8 reduce_sum.61
  114.9 426.5 %all-gather.16.cloned.1.call-done = f32[32768,128]{1,0:T(8,128)} async-done(((f32[128,128]{1,0:T(8,128)}), f32[32768,128]{1,0:T(8,128)}) %all-gather.16.cloned.1.call-update) | async-done | bytes 16777232 | tf_op jit(solution)/shard_map/while/body/eval_jaxpr/all_gather | solution.py:12
  541.4 6.6 reduce_sum.62
  548.1 11.7 cholesky.85
  561.2 9.8 custom-call.28
  573.1 130.9 %all-gather.18.cloned.1.call-done = f32[16,5,128,128]{3,2,1,0:T(8,128)} async-done(((f32[1,5,128,128]{3,2,1,0:T(8,128)}), f32[16,5,128,128]{3,2,1,0:T(8,128)}) %all-gather.18.cloned.1.call-update) | async-done | bytes 5242896 | tf_op jit(solution)/shard_map/while/body/eval_jaxpr/all_gather | solution.py:12
  704.0 2.8 reduce_sum.63
  711.0 48.4 %all-gather.14.cloned.1.call-done = f32[10240,128]{1,0:T(8,128)} async-done(((f32[640,128]{1,0:T(8,128)}), f32[10240,128]{1,0:T(8,128)}) %all-gather.14.cloned.1.call-update) | async-done | bytes 5242896 | tf_op jit(solution)/shard_map/while/body/eval_jaxpr/all_gather | solution.py:12
  759.4 2.8 reduce_sum.61
  762.1 426.4 %all-gather.16.cloned.1.call-done = f32[32768,128]{1,0:T(8,128)} async-done(((f32[128,128]{1,0:T(8,128)}), f32[32768,128]{1,0:T(8,128)}) %all-gather.16.cloned.1.call-update) | async-done | bytes 16777232 | tf_op jit(solution)/shard_map/while/body/eval_jaxpr/all_gather | solution.py:12
  1188.5 6.6 reduce_sum.62
  1195.2 11.7 cholesky.85
  1208.2 9.8 custom-call.28
  1220.2 130.9 %all-gather.18.cloned.1.call-done = f32[16,5,128,128]{3,2,1,0:T(8,128)} async-done(((f32[1,5,128,128]{3,2,1,0:T(8,128)}), f32[16,5,128,128]{3,2,1,0:T(8,128)}) %all-gather.18.cloned.1.call-update) | async-done | bytes 5242896 | tf_op jit(solution)/shard_map/while/body/eval_jaxpr/all_gather | solution.py:12
  1351.1 2.8 reduce_sum.63
  1358.0 48.7 %all-gather.14.cloned.1.call-done = f32[10240,128]{1,0:T(8,128)} async-done(((f32[640,128]{1,0:T(8,128)}), f32[10240,128]{1,0:T(8,128)}) %all-gather.14.cloned.1.call-update) | async-done | bytes 5242896 | tf_op jit(solution)/shard_map/while/body/eval_jaxpr/all_gather | solution.py:12
  1406.7 2.8 reduce_sum.61
  1409.5 426.5 %all-gather.16.cloned.1.call-done = f32[32768,128]{1,0:T(8,128)} async-done(((f32[128,128]{1,0:T(8,128)}), f32[32768,128]{1,0:T(8,128)}) %all-gather.16.cloned.1.call-update) | async-done | bytes 16777232 | tf_op jit(solution)/shard_map/while/body/eval_jaxpr/all_gather | solution.py:12
  1836.0 6.6 reduce_sum.62
  1842.7 11.7 cholesky.85
  1855.7 9.8 custom-call.28
  1867.7 130.9 %all-gather.18.cloned.1.call-done = f32[16,5,128,128]{3,2,1,0:T(8,128)} async-done(((f32[1,5,128,128]{3,2,1,0:T(8,128)}), f32[16,5,128,128]{3,2,1,0:T(8,128)}) %all-gather.18.cloned.1.call-update) | async-done | bytes 5242896 | tf_op jit(solution)/shard_map/while/body/eval_jaxpr/all_gather | solution.py:12
  1998.6 2.8 reduce_sum.63
  (83 shorter events, 25.7 us)
Async XLA Ops:
  9.8 7.3 copy-start.2
  9.8 31.0 %all-to-all-start = ((f32[2,3,2,128,384]{4,3,1,0,2:T(8,128)}), f32[2,3,2,128,384]{4,3,1,0,2:T(8,128)}, u32[]{:S(2)}, u32[]{:S(2)}) async-start(f32[2,3,2,128,384]{4,3,1,0,2:T(8,128)} %copy.23), calls=%async_computation | async-start | bytes 4718592 | tf_op jit(solution)/shard_map/all_to_all | solution.py:33
  54.3 6.3 copy-start.1
  61.3 50.8 %all-gather.14.cloned.1.call-start = ((), (), s32[]{:S(2)}) async-start(), calls=%async_computation.1 | async-start | bytes 5570560 | tf_op jit(solution)/shard_map/while/body/eval_jaxpr/all_gather | solution.py:12
  62.2 479.2 %all-gather.16.cloned.1.call-start = ((), (), s32[]{:S(2)}) async-start(), calls=%async_computation.2 | async-start | bytes 16842752 | tf_op jit(solution)/shard_map/while/body/eval_jaxpr/all_gather | solution.py:12
  62.9 641.1 %all-gather.18.cloned.1.call-start = ((), (), s32[]{:S(2)}) async-start(), calls=%async_computation.3 | async-start | bytes 5570560 | tf_op jit(solution)/shard_map/while/body/eval_jaxpr/all_gather | solution.py:12
  709.3 50.0 %all-gather.14.cloned.1.call-start = ((), (), s32[]{:S(2)}) async-start(), calls=%async_computation.1 | async-start | bytes 5570560 | tf_op jit(solution)/shard_map/while/body/eval_jaxpr/all_gather | solution.py:12
  710.2 478.3 %all-gather.16.cloned.1.call-start = ((), (), s32[]{:S(2)}) async-start(), calls=%async_computation.2 | async-start | bytes 16842752 | tf_op jit(solution)/shard_map/while/body/eval_jaxpr/all_gather | solution.py:12
  710.9 640.2 %all-gather.18.cloned.1.call-start = ((), (), s32[]{:S(2)}) async-start(), calls=%async_computation.3 | async-start | bytes 5570560 | tf_op jit(solution)/shard_map/while/body/eval_jaxpr/all_gather | solution.py:12
  1356.4 50.3 %all-gather.14.cloned.1.call-start = ((), (), s32[]{:S(2)}) async-start(), calls=%async_computation.1 | async-start | bytes 5570560 | tf_op jit(solution)/shard_map/while/body/eval_jaxpr/all_gather | solution.py:12
  1357.2 478.8 %all-gather.16.cloned.1.call-start = ((), (), s32[]{:S(2)}) async-start(), calls=%async_computation.2 | async-start | bytes 16842752 | tf_op jit(solution)/shard_map/while/body/eval_jaxpr/all_gather | solution.py:12
  1358.0 640.6 %all-gather.18.cloned.1.call-start = ((), (), s32[]{:S(2)}) async-start(), calls=%async_computation.3 | async-start | bytes 5570560 | tf_op jit(solution)/shard_map/while/body/eval_jaxpr/all_gather | solution.py:12
  2003.9 1.2 copy-start
Sparse Core Ops, SparseCore 0:
  64.0 48.1 all-gather.13
  114.0 427.3 all-gather.15
  572.6 131.3 all-gather.17
  711.7 47.6 all-gather.13
  761.1 427.3 all-gather.15
  1219.6 131.3 all-gather.17
  1359.0 47.6 all-gather.13
  1408.6 427.3 all-gather.15
  1867.2 131.3 all-gather.17
